TPU v7x, 128 devices: a whole 4x4x4 slice. The times are simulated.
128 devices in a mesh: dp: 32 (over x, z, core), mp: 4 (over y).
Axes of the slice: x: 4, y: 4, z: 4, core: 2. Of those that a mesh axis runs over, the one named last changes fastest.
Arguments:
- tokens: bfloat16 [32, 768, 1536], P('dp'), may hold values from -6 to 6
- lengths: int32 [32], P('dp'), may hold values from 1 to 768, as said below
- buckets: int32 [32], P('dp'), may hold values from 0 to 3, as said below
- out_cotangent: bfloat16 [32, 768, 1536], P('dp'), may hold values from -6 to 6
- gain_attn: bfloat16 [1536], replicated, may hold values from 0.5 to 1.5
- w_query: bfloat16 [1536, 1536], P(None, 'mp'), may hold values from -0.15625 to 0.15625
- w_key: bfloat16 [1536, 1536], P(None, 'mp'), may hold values from -0.15625 to 0.15625
- w_value: bfloat16 [1536, 1536], P(None, 'mp'), may hold values from -0.15625 to 0.15625
- w_outgate: bfloat16 [1536, 1536], P(None, 'mp'), may hold values from -0.15625 to 0.15625
- w_forget: bfloat16 [1536, 24], P(None, 'mp'), may hold values from -0.15625 to 0.15625
- b_forget: bfloat16 [24], P('mp'), may hold values from 1 to 7
- w_out: bfloat16 [1536, 1536], P('mp'), may hold values from -1.5 to 1.5
- gain_mlp: bfloat16 [1536], replicated, may hold values from 0.5 to 1.5
- w_gate: bfloat16 [1536, 4096], P(None, 'mp'), may hold values from -0.15625 to 0.15625
- w_up: bfloat16 [1536, 4096], P(None, 'mp'), may hold values from -0.15625 to 0.15625
- w_down: bfloat16 [4096, 1536], P('mp'), may hold values from -0.09375 to 0.09375
Outputs:
- output: bfloat16 [32, 768, 1536], P('dp')
- input_grad: float32 [32, 768, 1536], P('dp')
- grad_gain_attn: float32 [1536], P('dp')
- grad_query: float32 [1536, 1536], P('dp', 'mp')
- grad_key: float32 [1536, 1536], P('dp', 'mp')
- grad_value: float32 [1536, 1536], P('dp', 'mp')
- grad_outgate: float32 [1536, 1536], P('dp', 'mp')
- grad_forget: float32 [1536, 24], P('dp', 'mp')
- grad_bias: float32 [24], P('mp')
- grad_out: float32 [1536, 1536], P('mp', 'dp')
- grad_gain_mlp: float32 [1536], P('dp')
- grad_gate: float32 [1536, 4096], P('dp', 'mp')
- grad_up: float32 [1536, 4096], P('dp', 'mp')
- grad_down: float32 [4096, 1536], P('mp', 'dp')
- rms: float32 [3, 4], replicated
Inputs may be any that keep to these rules, and one draw needn't show every extreme that they name: `lengths`: A sequence with bucket id b has a length between b * 192 + 1 and (b + 1) * 192; some sequence has length 768. `buckets`: every bucket id occurs in every draw.
All inputs are finite; a program needn't handle non-finite values.
Results may differ from a plain program's by a relative error of at most 0.014.
Values sent between devices are 32-bit elements; how exact they have to be, the bound alone decides.
A program may use at most 256 MiB of HBM per device.

v0:
```python
import math
import jax
import jax.numpy as jnp
from jax import lax
from jax.sharding import PartitionSpec as P

NBUCKET = 4
EPSILON = 1e-06


def sent_together(arrays, axis, dim, along):
    widths = [math.prod(a.shape[along:]) for a in arrays]
    both = jnp.concatenate(
        [a.reshape(*a.shape[:along], w) for a, w in zip(arrays, widths)], axis=along
    )
    filled = lax.psum_scatter(both, axis, scatter_dimension=dim, tiled=True)
    tiles = jnp.split(filled, [sum(widths[:k]) for k in range(1, len(widths))], axis=along)
    return tuple(
        (b.reshape(*filled.shape[:along], *a.shape[along:]) for a, b in zip(arrays, tiles))
    )


def side_by_side(arrays, axis, dim, along):
    both = jnp.concatenate(arrays, axis=along)
    filled, at, done = (lax.psum_scatter(both, axis, scatter_dimension=dim, tiled=True), 0, [])
    for a in arrays:
        done.append(lax.slice_in_dim(filled, at, at + a.shape[along], axis=along))
        at += a.shape[along]
    return tuple(done)


def sent_to_all(array, axis):
    devices = lax.axis_size(axis)
    return lax.all_to_all(
        jnp.broadcast_to(array[None], (devices, *array.shape)), axis, 0, 0, tiled=True
    )


def over_copies(array, axis):
    return sent_to_all(array, axis).sum(axis=0)


def in_one(arrays, axis):
    ends = [0]
    for a in arrays:
        ends.append(ends[-1] + a.size)
    subtotal = over_copies(jnp.concatenate([a.ravel() for a in arrays]), axis)
    return tuple((subtotal[b:e].reshape(a.shape) for a, b, e in zip(arrays, ends, ends[1:])))


def norm_rows(values):
    return values * lax.rsqrt(jnp.mean(values * values, axis=-1, keepdims=True) + EPSILON)


def gain_norm(values, gain_row):
    return norm_rows(values) * gain_row


def swiglu(gate_pre, up_pre):
    return jax.nn.silu(gate_pre) * up_pre


def low_dot(left, right):
    return jnp.dot(left, right, preferred_element_type=jnp.float32)


def back_dot(left, right):
    return lax.dot_general(
        left, right, (((0,), (0,)), ((), ())), preferred_element_type=jnp.float32
    )


def trans_dot(left, right):
    return lax.dot_general(
        left, right, (((1,), (1,)), ((), ())), preferred_element_type=jnp.float32
    )


def per_device(
    tokens,
    lengths,
    buckets,
    out_cotangent,
    gain_attn,
    w_query,
    w_key,
    w_value,
    w_outgate,
    w_forget,
    b_forget,
    w_out,
    gain_mlp,
    w_gate,
    w_up,
    w_down,
):
    inputs = tokens[0].astype(jnp.float32)
    seq_len, model_width = inputs.shape
    head_count = w_forget.shape[1]
    head_dim = w_query.shape[1] // head_count
    score_scale = head_dim ** (-0.5)
    valid_len = lengths[0]
    positions = jnp.arange(seq_len)
    valid_rows = (positions < valid_len).astype(jnp.float32)[:, None]
    allowed = (positions[None, :] <= positions[:, None]) & (positions[None, :] < valid_len)
    normed_in, norm_back_in = jax.vjp(gain_norm, inputs, gain_attn.astype(jnp.float32))
    in_low = normed_in.astype(jnp.bfloat16)
    query_pre = low_dot(in_low, w_query)
    key_pre = low_dot(in_low, w_key)
    value_pre = low_dot(in_low, w_value)
    outgate_pre = low_dot(in_low, w_outgate)
    forget_pre = low_dot(in_low, w_forget) + b_forget.astype(jnp.float32)
    query_norm, query_back = jax.vjp(norm_rows, query_pre.reshape(seq_len, head_count, head_dim))
    key_norm, key_back = jax.vjp(norm_rows, key_pre.reshape(seq_len, head_count, head_dim))
    query_low = query_norm.astype(jnp.bfloat16)
    key_low = key_norm.astype(jnp.bfloat16)
    value_low = value_pre.astype(jnp.bfloat16).reshape(seq_len, head_count, head_dim)
    log_decay = jnp.cumsum(jax.nn.log_sigmoid(forget_pre), axis=0).T

    def masked_scores():
        base_scores = (
            jnp.einsum("ihd,jhd->hij", query_low, key_low, preferred_element_type=jnp.float32)
            * score_scale
        )
        base_scores = base_scores + log_decay[:, :, None] - log_decay[:, None, :]
        return jnp.where(allowed[None], base_scores, -1e30)

    masked = masked_scores()
    row_top = jnp.max(masked, axis=-1, keepdims=True)
    exponent = jnp.exp(masked - row_top)
    row_total = jnp.sum(exponent, axis=-1, keepdims=True)
    attn_probs = exponent / row_total
    log_total = row_top + jnp.log(row_total)
    attended = jnp.einsum(
        "hij,jhd->ihd",
        attn_probs.astype(jnp.bfloat16),
        value_low,
        preferred_element_type=jnp.float32,
    ).reshape(seq_len, head_count * head_dim)
    gate_sig = jax.nn.sigmoid(outgate_pre)
    gated_low = (attended * gate_sig).astype(jnp.bfloat16)
    branch_attn = lax.psum(low_dot(gated_low, w_out), "mp")
    middle = inputs + branch_attn
    normed_mid, norm_back_mid = jax.vjp(gain_norm, middle, gain_mlp.astype(jnp.float32))
    mid_low = normed_mid.astype(jnp.bfloat16)
    gate_pre = low_dot(mid_low, w_gate)
    up_pre = low_dot(mid_low, w_up)
    hidden_f, swiglu_back = jax.vjp(swiglu, gate_pre, up_pre)
    hidden_low = hidden_f.astype(jnp.bfloat16)
    branch_mlp = lax.psum(low_dot(hidden_low, w_down), "mp")
    layer_out = (middle + branch_mlp).astype(jnp.bfloat16)
    bucket_hot = (buckets[0] == jnp.arange(NBUCKET)).astype(jnp.float32)
    square_sums = jnp.stack(
        [
            jnp.sum(valid_rows * inputs * inputs),
            jnp.sum(valid_rows * branch_attn * branch_attn),
            jnp.sum(valid_rows * branch_mlp * branch_mlp),
        ]
    )
    bucket_sums = square_sums[:, None] * bucket_hot[None, :]
    bucket_count = valid_len.astype(jnp.float32) * bucket_hot
    grad_rows = out_cotangent[0].astype(jnp.float32) * valid_rows
    grad_rows_low = grad_rows.astype(jnp.bfloat16)
    grad_w_down = back_dot(hidden_low, grad_rows_low)
    grad_hidden = trans_dot(grad_rows_low, w_down)
    grad_gate_f, grad_up_f = swiglu_back(grad_hidden)
    gate_grad_low = grad_gate_f.astype(jnp.bfloat16)
    up_grad_low = grad_up_f.astype(jnp.bfloat16)
    grad_w_gate = back_dot(mid_low, gate_grad_low)
    grad_w_up = back_dot(mid_low, up_grad_low)
    grad_mid_norm = lax.psum(trans_dot(gate_grad_low, w_gate) + trans_dot(up_grad_low, w_up), "mp")
    grad_middle_part, grad_gain_mlp = norm_back_mid(grad_mid_norm)
    grad_middle = grad_rows + grad_middle_part
    middle_low = grad_middle.astype(jnp.bfloat16)
    grad_w_out = back_dot(gated_low, middle_low)
    grad_gated = trans_dot(middle_low, w_out)
    attended_grad_low = (grad_gated * gate_sig).astype(jnp.bfloat16)
    outgate_grad_low = (grad_gated * attended * gate_sig * (1.0 - gate_sig)).astype(jnp.bfloat16)
    attended_heads = attended_grad_low.reshape(seq_len, head_count, head_dim)
    again_probs = jnp.exp(masked_scores() - log_total)
    grad_probs = jnp.einsum(
        "ihd,jhd->hij", attended_heads, value_low, preferred_element_type=jnp.float32
    )
    row_delta = jnp.sum(again_probs * grad_probs, axis=-1, keepdims=True)
    scores_grad_low = (again_probs * (grad_probs - row_delta)).astype(jnp.bfloat16)
    value_grad_low = (
        jnp.einsum(
            "hij,ihd->jhd",
            again_probs.astype(jnp.bfloat16),
            attended_heads,
            preferred_element_type=jnp.float32,
        )
        .reshape(seq_len, head_count * head_dim)
        .astype(jnp.bfloat16)
    )
    grad_query_norm = (
        jnp.einsum("hij,jhd->ihd", scores_grad_low, key_low, preferred_element_type=jnp.float32)
        * score_scale
    )
    grad_key_norm = (
        jnp.einsum("hij,ihd->jhd", scores_grad_low, query_low, preferred_element_type=jnp.float32)
        * score_scale
    )
    score_grad = scores_grad_low.astype(jnp.float32)
    grad_decay = jnp.sum(score_grad, axis=2) - jnp.sum(score_grad, axis=1)
    grad_log_forget = jnp.flip(jnp.cumsum(jnp.flip(grad_decay, 1), axis=1), 1).T
    forget_grad_low = (grad_log_forget * jax.nn.sigmoid(-forget_pre)).astype(jnp.bfloat16)
    query_grad_low = (
        query_back(grad_query_norm)[0].reshape(seq_len, head_count * head_dim).astype(jnp.bfloat16)
    )
    key_grad_low = (
        key_back(grad_key_norm)[0].reshape(seq_len, head_count * head_dim).astype(jnp.bfloat16)
    )
    grad_w_query = back_dot(in_low, query_grad_low)
    grad_w_key = back_dot(in_low, key_grad_low)
    grad_w_value = back_dot(in_low, value_grad_low)
    grad_w_outgate = back_dot(in_low, outgate_grad_low)
    grad_w_forget = back_dot(in_low, forget_grad_low)
    grad_b_forget = jnp.sum(forget_grad_low.astype(jnp.float32), axis=0)
    grad_in_local = (
        trans_dot(query_grad_low, w_query)
        + trans_dot(key_grad_low, w_key)
        + trans_dot(value_grad_low, w_value)
    )
    grad_in_local = (
        grad_in_local
        + trans_dot(outgate_grad_low, w_outgate)
        + trans_dot(forget_grad_low, w_forget)
    )
    grad_in_norm = lax.psum(grad_in_local, "mp")
    grad_in_part, grad_gain_attn = norm_back_in(grad_in_norm)
    input_grad = grad_middle + grad_in_part
    all_shares = (
        *sent_together(
            (grad_gain_attn, grad_w_query, grad_w_key, grad_w_value, grad_w_outgate, grad_w_forget),
            "dp",
            0,
            1,
        ),
        lax.psum_scatter(grad_w_out, "dp", scatter_dimension=1, tiled=True),
        *side_by_side((grad_w_gate, grad_w_up), "dp", 0, 1),
        lax.psum_scatter(grad_w_down, "dp", scatter_dimension=1, tiled=True),
        lax.psum_scatter(grad_gain_mlp, "dp", scatter_dimension=0, tiled=True),
    )
    attn_shares = all_shares[:7]
    mlp_shares = all_shares[7:]
    bucket_total, bucket_rows, bias_sum = in_one((bucket_sums, bucket_count, grad_b_forget), "dp")
    rms = jnp.sqrt(bucket_total / (bucket_rows[None, :] * model_width))
    return (
        layer_out[None],
        input_grad[None],
        attn_shares[0],
        attn_shares[1],
        attn_shares[2],
        attn_shares[3],
        attn_shares[4],
        attn_shares[5],
        bias_sum,
        attn_shares[6],
        mlp_shares[3],
        mlp_shares[0],
        mlp_shares[1],
        mlp_shares[2],
        rms,
    )


def solution(mesh):
    placed = (
        P("dp", None, None),
        P("dp"),
        P("dp"),
        P("dp", None, None),
        P(),
        P(None, "mp"),
        P(None, "mp"),
        P(None, "mp"),
        P(None, "mp"),
        P(None, "mp"),
        P("mp"),
        P("mp", None),
        P(),
        P(None, "mp"),
        P(None, "mp"),
        P("mp", None),
    )
    return jax.shard_map(
        per_device,
        mesh=mesh,
        in_specs=placed,
        out_specs=(
            P("dp", None, None),
            P("dp", None, None),
            P("dp"),
            P("dp", "mp"),
            P("dp", "mp"),
            P("dp", "mp"),
            P("dp", "mp"),
            P("dp", "mp"),
            P("mp"),
            P("mp", "dp"),
            P("dp"),
            P("dp", "mp"),
            P("dp", "mp"),
            P("mp", "dp"),
            P(),
        ),
        check_vma=False,
    )
```

profile of v0, /device:TPU:0, one launch (start us, length us, event | category | flops | bytes accessed | tf_op | source)
XLA Modules:
  0.0 918.8 jit_solution(12748875508411315006)
XLA Ops:
  18.3 4.2 multiply_reduce_fusion.7
  30.5 7.2 fusion.82
  37.6 6.9 fusion
  44.6 6.5 fusion.5
  58.5 103.3 %all-reduce.6.cloned.1.call-done = f32[768,1536]{1,0:T(8,128)} async-done(((f32[768,1536]{1,0:T(8,128)}), f32[768,1536]{1,0:T(8,128)}) %all-reduce.6.cloned.1.call-update) | async-done | bytes 4718608 | tf_op jit(solution)/shard_map/psum | solution.py:142
  161.8 3.8 multiply_reduce_fusion.3
  174.6 4.9 multiply_convert_fusion.2
  182.2 4.4 convolution_add_fusion
  187.1 5.6 fusion.86
  192.7 95.3 %all-reduce.8.cloned.1.call-done = f32[768,1536]{1,0:T(8,128)} async-done(((f32[768,1536]{1,0:T(8,128)}), f32[768,1536]{1,0:T(8,128)}) %all-reduce.8.cloned.1.call-update) | async-done | bytes 4718608 | tf_op jit(solution)/shard_map/psum | solution.py:171
  288.0 5.0 multiply_reduce_fusion.1
  293.9 3.7 fusion.19
  303.5 6.5 multiply_reduce_fusion
  310.1 9.8 %convert_reduce_fusion = (f32[6,768]{1,0:T(8,128)S(1)}, f32[6,768]{1,0:T(8,128)S(1)}, bf16[6,768,768]{1,2,0:T(8,128)(2,1)}) fusion(f32[6,768,768]{1,2,0:T(8,128)} %get-tuple-element.151, f32[6,768]{1,0:T(8,128)S(1)} %get-tuple-element.150, f32[6,768,768]{1,2,0:T(8,128)S(1)} %bitcast.193, f32[6,768]{1,0:T(8,128)S(1)} %log_add_fusion), kind=kLoop, calls=%fused_computation | loop fusion | flops 24763392 | bytes 35463168 | tf_op jit(solution)/shard_map/reduce_sum | solution.py:205
  319.9 6.3 multiply_reduce_fusion.4
  326.1 5.3 multiply_reduce_fusion.5
  353.4 6.2 fusion.93
  359.6 4.6 fusion.94
  364.2 10.5 %pad_maximum_fusion = f32[1536,2048]{0,1:T(8,128)} fusion(f32[1536,1024]{0,1:T(8,128)} %fusion.94, f32[1536,1024]{0,1:T(8,128)} %fusion.93), kind=kLoop, calls=%fused_computation.8 | loop fusion | flops 3145728 | bytes 25165824 | tf_op jit(solution)/shard_map/concatenate | solution.py:24
  374.7 12.7 %copy.111 = f32[1536,2048]{1,0:T(8,128)} copy(f32[1536,2048]{0,1:T(8,128)} %pad_maximum_fusion) | data formatting | bytes 25165824
  401.1 128.1 %all-reduce.10.cloned.1.call-done = (f32[768,1536]{1,0:T(8,128)}, f32[768,1536]{1,0:T(8,128)}) async-done(((f32[768,1536]{1,0:T(8,128)}, f32[768,1536]{1,0:T(8,128)}), (f32[768,1536]{1,0:T(8,128)}, f32[768,1536]{1,0:T(8,128)})) %all-reduce.10.cloned.1.call-update) | async-done | bytes 9437200 | tf_op jit(solution)/shard_map/psum | solution.py:150
  529.3 10.4 %fusion.23 = (f32[]{:T(128)}, f32[]{:T(128)}, bf16[1,768,1536]{2,1,0:T(8,128)(2,1)}, f32[]{:T(128)}, f32[768]{0:T(1024)S(1)}, /*index=5*/f32[1536]{0:T(1024)S(1)}) fusion(f32[768,1536]{1,0:T(8,128)} %all-reduce.6.cloned.1.call-done, f32[768]{0:T(1024)S(1)} %fusion.72, f32[768,1536]{1,0:T(8,128)} %get-tuple-element.114, f32[768,1536]{1,0:T(8,128)} %copy-done.2, ...), kind=kLoop, calls=%fused_computation.39 | loop fusion | flops 21231356 | bytes 23614476 | tf_op jit(solution)/shard_map/reduce_sum | solution.py:156
  539.7 34.5 %concatenate.9 = f32[1536,1543]{0,1:T(8,128)} concatenate(f32[1536,1]{0,1:T(1,128)S(1)} %reshape.318, f32[1536,384]{0,1:T(8,128)} %fusion.37, f32[1536,384]{0,1:T(8,128)} %fusion.39, f32[1536,384]{0,1:T(8,128)} %fusion.35, f32[1536,384]{0,1:T(8,128)} %fusion.95, f32[1536,6]{0,1:T(8,128)S(1)} %fusion.92), dimensions={1} | concatenate | bytes 18960384 | tf_op jit(solution)/shard_map/concatenate | solution.py:13
  574.2 10.6 %copy.109 = f32[1536,1543]{1,0:T(8,128)} copy(f32[1536,1543]{0,1:T(8,128)} %concatenate.9) | data formatting | bytes 18960384
  586.0 5.3 fusion.54
  591.4 6.2 fusion.58
  599.5 69.3 %all-reduce = f32[1536]{0:T(1024)S(1)} all-reduce(f32[1536]{0:T(1024)S(1)} %get-tuple-element.105), channel_id=4, replica_groups=mesh['dp'=32,'mp'=4] {'dp'}, use_global_device_ids=true, to_apply=%region_30.31.clone | all-reduce | flops 1536 | bytes 12288
  672.3 3.8 all-to-all-start
  676.2 8.4 fusion.21
  687.8 50.7 %reduce-scatter.13.cloned.1.call-done = f32[48,1543]{1,0:T(8,128)} async-done(((f32[1536,1543]{1,0:T(8,128)}), f32[48,1543]{1,0:T(8,128)}) %reduce-scatter.13.cloned.1.call-update) | async-done | bytes 296272
  743.2 78.4 %reduce-scatter.9.cloned.1.call-done = f32[384,48]{0,1:T(8,128)} async-done(((f32[384,1536]{0,1:T(8,128)}), f32[384,48]{0,1:T(8,128)}) %reduce-scatter.9.cloned.1.call-update) | async-done | bytes 73744 | tf_op jit(solution)/shard_map/reduce_scatter | solution.py:240
  821.5 90.0 %reduce-scatter.11.cloned.1.call-done = f32[1024,48]{0,1:T(8,128)} async-done(((f32[1024,1536]{0,1:T(8,128)}), f32[1024,48]{0,1:T(8,128)}) %reduce-scatter.11.cloned.1.call-update) | async-done | bytes 196624 | tf_op jit(solution)/shard_map/reduce_scatter | solution.py:242
  (215 shorter events, 93.2 us)
Async XLA Ops:
  7.2 167.4 %copy-start = (bf16[1024,1536]{1,0:T(8,128)(2,1)S(1)}, bf16[1024,1536]{1,0:T(8,128)(2,1)}, u32[]{:S(2)}) copy-start(bf16[1024,1536]{1,0:T(8,128)(2,1)} %param.31) | copy-start | bytes 9437188
  7.2 5.9 copy-start.44
  7.2 154.6 %all-reduce.6.cloned.1.call-start = ((), (), s32[]{:S(2)}) async-start(), calls=%async_computation.5 | async-start | bytes 9437184 | tf_op jit(solution)/shard_map/psum | solution.py:142
  7.3 3.8 copy-start.4
  9.6 15.2 %copy-start.45 = (f32[768]{0:T(1024)}, f32[768]{0:T(1024)S(1)}, u32[]{:S(2)}) copy-start(f32[768]{0:T(1024)S(1)} %fusion.70) | copy-start | bytes 9220
  10.3 14.5 %copy-start.42 = (f32[1536]{0:T(1024)}, f32[1536]{0:T(1024)S(1)}, u32[]{:S(2)}) copy-start(f32[1536]{0:T(1024)S(1)} %convert_element_type.141) | copy-start | bytes 18436
  24.9 4.3 copy-start.7
  24.9 4.3 copy-start.36
  30.3 14.2 %copy-start.40 = (bf16[768,384]{0,1:T(8,128)(2,1)}, bf16[768,384]{0,1:T(8,128)(2,1)S(1)}, u32[]{:S(2)}) copy-start(bf16[768,384]{0,1:T(8,128)(2,1)S(1)} %convolution_convert_fusion) | copy-start | bytes 1769476
  44.6 6.5 copy-start.38
  57.9 230.1 %all-reduce.8.cloned.1.call-start = ((), (), s32[]{:S(2)}) async-start(), calls=%async_computation.6 | async-start | bytes 9437184 | tf_op jit(solution)/shard_map/psum | solution.py:171
  186.6 342.6 %all-reduce.10.cloned.1.call-start = ((), (), s32[]{:S(2)}) async-start(), calls=%async_computation.11 | async-start | bytes 18874368 | tf_op jit(solution)/shard_map/psum | solution.py:150
  288.0 5.1 copy-start.10
  288.0 5.9 copy-start.29
  293.8 3.7 copy-start.34
  293.9 3.7 copy-start.35
  293.9 6.4 slice-start
  293.9 7.8 slice-start.1
  293.9 9.0 slice-start.2
  297.6 5.9 slice-start.3
  297.6 5.9 copy-start.41
  310.1 9.8 %copy-start.12 = (f32[768,6,64]{0,2,1:T(8,128)S(1)}, f32[768,6,64]{0,2,1:T(8,128)}, u32[]{:S(2)}) copy-start(f32[768,6,64]{0,2,1:T(8,128)} %get-tuple-element.143) | copy-start | bytes 3538948
  310.1 9.8 %copy-start.14 = (f32[768,6,64]{0,2,1:T(8,128)S(1)}, f32[768,6,64]{0,2,1:T(8,128)}, u32[]{:S(2)}) copy-start(f32[768,6,64]{0,2,1:T(8,128)} %copy-done.13) | copy-start | bytes 3538948
  351.7 334.3 %reduce-scatter.15.cloned.1.call-start = ((), (), s32[]{:S(2)}) async-start(), calls=%async_computation.10 | async-start | bytes 12976128
  353.4 6.2 copy-start.54
  387.4 351.1 %reduce-scatter.13.cloned.1.call-start = ((), (), s32[]{:S(2)}) async-start(), calls=%async_computation.9 | async-start | bytes 10543104
  584.8 6.6 copy-start.30
  584.8 236.7 %reduce-scatter.9.cloned.1.call-start = ((), (), s32[]{:S(2)}) async-start(), calls=%async_computation.7 | async-start | bytes 2433024 | tf_op jit(solution)/shard_map/reduce_scatter | solution.py:240
  591.3 320.2 %reduce-scatter.11.cloned.1.call-start = ((), (), s32[]{:S(2)}) async-start(), calls=%async_computation.8 | async-start | bytes 6488064 | tf_op jit(solution)/shard_map/reduce_scatter | solution.py:242
  597.6 78.6 %copy-start.48 = (f32[768]{0:T(1024)S(1)}, f32[768]{0:T(1024)}, u32[]{:S(2)}) copy-start(f32[768]{0:T(1024)} %copy-done.47) | copy-start | bytes 9220
  672.3 12.3 %all-to-all-start = ((f32[32,1,22]{2,1,0:T(1,128)}), f32[32,1,22]{2,1,0:T(1,128)S(1)}, u32[]{:S(2)}, u32[]{:S(2)}) async-start(f32[32,1,22]{2,1,0:T(1,128)} %broadcast_in_dim.38), calls=%async_computation | async-start | bytes 32768 | tf_op jit(solution)/shard_map/all_to_all | solution.py:34
  676.2 235.4 %copy-start.1 = (bf16[1024,1536]{1,0:T(8,128)(2,1)S(1)}, bf16[1024,1536]{1,0:T(8,128)(2,1)}, u32[]{:S(2)}) copy-start(bf16[1024,1536]{1,0:T(8,128)(2,1)} %param.31) | copy-start | bytes 9437188
  (36 other events, 77.1 us)
Sparse Core Ops, SparseCore 0:
  58.0 103.7 all-reduce.5
  186.7 101.2 all-reduce.7
  351.9 177.3 all-reduce.9
  533.0 104.4 reduce-scatter.14
  641.6 96.8 reduce-scatter.12
  742.9 78.5 reduce-scatter.8
  825.9 85.6 reduce-scatter.10
where the time goes:
time: 930 us; the launch traced here: 919 us
  waiting for transfers between devices  546 us (59%)
  matrix products  119 us (13%)
  local copies, waits for them, and re-layouts  90.5 us (10%)
  other arithmetic  72.1 us (8%)
  blocking collectives  69.3 us (7%)
  between operations  17.2 us (2%)
    psum x1, waiting for transfers between devices, per_device(): branch_mlp = lax.psum(low_dot(hidden_low, w_down), 'mp')  128 us
    psum x1, waiting for transfers between devices, per_device(): branch_attn = lax.psum(low_dot(gated_low, w_out), 'mp')  103 us
    psum x1, waiting for transfers between devices, per_device(): lax.psum(trans_dot(gate_grad_low, w_gate) + trans_dot(up_grad_low, w_up),...  95.3 us
    reduce_scatter x1, waiting for transfers between devices, per_device(): lax.psum_scatter(grad_w_down, 'dp', scatter_dimension=1, tiled=True)  90 us
    reduce_scatter x1, waiting for transfers between devices, per_device(): lax.psum_scatter(grad_w_out, 'dp', scatter_dimension=1, tiled=True)  78.4 us
    unnamed x1, blocking collectives  69.3 us
    unnamed x9, waiting for transfers between devices  50.8 us
    unnamed x130, local copies, waits for them, and re-layouts  48 us
  transfers between devices with their start and end apart: 8, of which 6 were waited for; matrix products, arithmetic and copies ran while one was open for 15% of the time, Pallas kernels for 0%

commit v1 on v0

--- a/solution.py
+++ b/solution.py
@@ -139,7 +139,9 @@
     ).reshape(seq_len, head_count * head_dim)
     gate_sig = jax.nn.sigmoid(outgate_pre)
     gated_low = (attended * gate_sig).astype(jnp.bfloat16)
-    branch_attn = lax.psum(low_dot(gated_low, w_out), "mp")
+    x_part = low_dot(gated_low, w_out)
+    piece_out = lax.all_gather(x_part, axis_name="mp")
+    branch_attn = jnp.sum(piece_out, 0)
     middle = inputs + branch_attn
     normed_mid, norm_back_mid = jax.vjp(gain_norm, middle, gain_mlp.astype(jnp.float32))
     mid_low = normed_mid.astype(jnp.bfloat16)

time: 930 us -> 1010 us (1.086)
  waiting for transfers between devices: 546 us -> 617 us
  other arithmetic: 72.1 us -> 83.4 us
    all_gather x0 -> x1, waiting for transfers between devices: none -> 174 us  [per_device(): piece_out = lax.all_gather(x_part, axis_name='mp')]
    psum x1 -> x0, waiting for transfers between devices: 103 us -> none  [per_device(): branch_attn = lax.psum(low_dot(gated_low, w_out), 'mp')]
    reduce_sum x0 -> x1, other arithmetic: none -> 11.3 us  [per_device(): branch_attn = jnp.sum(piece_out, 0)]
  transfers between devices with their start and end apart: 8 -> 8, of which waited for: 6 -> 6; matrix products, arithmetic and copies ran while one was open for 15% -> 14% of each run, Pallas kernels for 0% -> 0%
where the time goes in v1:
time: 1010 us; the launch traced here: 1000 us
  waiting for transfers between devices  617 us (61%)
  matrix products  119 us (12%)
  local copies, waits for them, and re-layouts  90.3 us (9%)
  other arithmetic  83.4 us (8%)
  blocking collectives  69.4 us (7%)
  between operations  17.3 us (2%)
    all_gather x1, waiting for transfers between devices, per_device(): piece_out = lax.all_gather(x_part, axis_name='mp')  174 us
    psum x1, waiting for transfers between devices, per_device(): branch_mlp = lax.psum(low_dot(hidden_low, w_down), 'mp')  128 us
    psum x1, waiting for transfers between devices, per_device(): lax.psum(trans_dot(gate_grad_low, w_gate) + trans_dot(up_grad_low, w_up),...  95.6 us
    reduce_scatter x1, waiting for transfers between devices, per_device(): lax.psum_scatter(grad_w_down, 'dp', scatter_dimension=1, tiled=True)  90 us
    reduce_scatter x1, waiting for transfers between devices, per_device(): lax.psum_scatter(grad_w_out, 'dp', scatter_dimension=1, tiled=True)  78.4 us
    unnamed x1, blocking collectives  69.4 us
    unnamed x9, waiting for transfers between devices  50.6 us
    unnamed x130, local copies, waits for them, and re-layouts  47.9 us
  transfers between devices with their start and end apart: 8, of which 6 were waited for; matrix products, arithmetic and copies ran while one was open for 14% of the time, Pallas kernels for 0%

profile of v1, /device:TPU:0, one launch (start us, length us, event | category | flops | bytes accessed | tf_op | source)
XLA Modules:
  0.0 1001.5 jit_solution(9092036079717061158)
XLA Ops:
  18.3 4.2 multiply_reduce_fusion.7
  30.5 7.3 fusion.82
  37.7 6.9 fusion
  44.7 6.5 fusion.5
  58.6 174.4 %all-gather.3.cloned.1.call-done = f32[3072,1536]{1,0:T(8,128)} async-done(((f32[768,1536]{1,0:T(8,128)}), f32[3072,1536]{1,0:T(8,128)}) %all-gather.3.cloned.1.call-update) | async-done | bytes 18874384 | tf_op jit(solution)/shard_map/all_gather | solution.py:143
  233.0 11.3 %reduce_sum.208 = f32[768,1536]{1,0:T(8,128)} reduce(f32[4,768,1536]{2,1,0:T(8,128)} %bitcast.194, f32[]{:T(128)} %constant.18.clone.1), dimensions={0}, to_apply=%region_7.8 | reduce | flops 3538944 | bytes 23592964 | tf_op jit(solution)/shard_map/reduce_sum | solution.py:144
  244.3 3.8 multiply_reduce_fusion.3
  257.1 4.9 multiply_convert_fusion.2
  264.7 4.4 convolution_add_fusion
  269.2 5.8 fusion.86
  275.0 95.6 %all-reduce.5.cloned.1.call-done = f32[768,1536]{1,0:T(8,128)} async-done(((f32[768,1536]{1,0:T(8,128)}), f32[768,1536]{1,0:T(8,128)}) %all-reduce.5.cloned.1.call-update) | async-done | bytes 4718608 | tf_op jit(solution)/shard_map/psum | solution.py:173
  370.6 5.0 multiply_reduce_fusion.1
  386.2 6.5 multiply_reduce_fusion
  392.7 9.8 convert_reduce_fusion
  402.5 6.3 multiply_reduce_fusion.4
  408.8 5.3 multiply_reduce_fusion.5
  436.1 6.2 fusion.93
  442.3 4.7 fusion.94
  447.0 10.4 %pad_maximum_fusion = f32[1536,2048]{0,1:T(8,128)} fusion(f32[1536,1024]{0,1:T(8,128)} %fusion.94, f32[1536,1024]{0,1:T(8,128)} %fusion.93), kind=kLoop, calls=%fused_computation.8 | loop fusion | flops 3145728 | bytes 25165824 | tf_op jit(solution)/shard_map/concatenate | solution.py:24
  457.4 12.7 %copy.111 = f32[1536,2048]{1,0:T(8,128)} copy(f32[1536,2048]{0,1:T(8,128)} %pad_maximum_fusion) | data formatting | bytes 25165824
  483.9 128.1 %all-reduce.7.cloned.1.call-done = (f32[768,1536]{1,0:T(8,128)}, f32[768,1536]{1,0:T(8,128)}) async-done(((f32[768,1536]{1,0:T(8,128)}, f32[768,1536]{1,0:T(8,128)}), (f32[768,1536]{1,0:T(8,128)}, f32[768,1536]{1,0:T(8,128)})) %all-reduce.7.cloned.1.call-update) | async-done | bytes 9437200 | tf_op jit(solution)/shard_map/psum | solution.py:152
  612.0 10.4 %fusion.23 = (f32[]{:T(128)}, f32[]{:T(128)}, bf16[1,768,1536]{2,1,0:T(8,128)(2,1)}, f32[]{:T(128)}, f32[768]{0:T(1024)S(1)}, /*index=5*/f32[1536]{0:T(1024)S(1)}) fusion(f32[768,1536]{1,0:T(8,128)} %reduce_sum.208, f32[768]{0:T(1024)S(1)} %get-tuple-element.157, f32[768,1536]{1,0:T(8,128)} %get-tuple-element.114, f32[768,1536]{1,0:T(8,128)} %copy-done.2, ...), kind=kLoop, calls=%fused_computation.39 | loop fusion | flops 21231356 | bytes 23614476 | tf_op jit(solution)/shard_map/reduce_sum | solution.py:158
  622.4 34.5 %concatenate.9 = f32[1536,1543]{0,1:T(8,128)} concatenate(f32[1536,1]{0,1:T(1,128)S(1)} %reshape.318, f32[1536,384]{0,1:T(8,128)} %fusion.37, f32[1536,384]{0,1:T(8,128)} %fusion.39, f32[1536,384]{0,1:T(8,128)} %fusion.35, f32[1536,384]{0,1:T(8,128)} %fusion.95, f32[1536,6]{0,1:T(8,128)S(1)} %fusion.92), dimensions={1} | concatenate | bytes 18960384 | tf_op jit(solution)/shard_map/concatenate | solution.py:13
  656.9 10.7 %copy.109 = f32[1536,1543]{1,0:T(8,128)} copy(f32[1536,1543]{0,1:T(8,128)} %concatenate.9) | data formatting | bytes 18960384
  668.8 5.2 fusion.54
  674.1 6.3 fusion.58
  682.4 69.4 %all-reduce = f32[1536]{0:T(1024)S(1)} all-reduce(f32[1536]{0:T(1024)S(1)} %get-tuple-element.105), channel_id=5, replica_groups=mesh['dp'=32,'mp'=4] {'dp'}, use_global_device_ids=true, to_apply=%region_30.31.clone | all-reduce | flops 1536 | bytes 12288
  755.2 3.8 all-to-all-start
  759.1 8.4 fusion.21
  770.7 50.5 %reduce-scatter.13.cloned.1.call-done = f32[48,1543]{1,0:T(8,128)} async-done(((f32[1536,1543]{1,0:T(8,128)}), f32[48,1543]{1,0:T(8,128)}) %reduce-scatter.13.cloned.1.call-update) | async-done | bytes 296272
  825.8 78.4 %reduce-scatter.9.cloned.1.call-done = f32[384,48]{0,1:T(8,128)} async-done(((f32[384,1536]{0,1:T(8,128)}), f32[384,48]{0,1:T(8,128)}) %reduce-scatter.9.cloned.1.call-update) | async-done | bytes 73744 | tf_op jit(solution)/shard_map/reduce_scatter | solution.py:242
  904.2 90.0 %reduce-scatter.11.cloned.1.call-done = f32[1024,48]{0,1:T(8,128)} async-done(((f32[1024,1536]{0,1:T(8,128)}), f32[1024,48]{0,1:T(8,128)}) %reduce-scatter.11.cloned.1.call-update) | async-done | bytes 196624 | tf_op jit(solution)/shard_map/reduce_scatter | solution.py:244
  (215 shorter events, 96.6 us)
Async XLA Ops:
  7.2 249.9 %copy-start = (bf16[1024,1536]{1,0:T(8,128)(2,1)S(1)}, bf16[1024,1536]{1,0:T(8,128)(2,1)}, u32[]{:S(2)}) copy-start(bf16[1024,1536]{1,0:T(8,128)(2,1)} %param.31) | copy-start | bytes 9437188
  7.2 5.9 copy-start.44
  7.2 225.8 %all-gather.3.cloned.1.call-start = ((), (), s32[]{:S(2)}) async-start(), calls=%async_computation.8 | async-start | bytes 23592960 | tf_op jit(solution)/shard_map/all_gather | solution.py:143
  7.3 3.8 copy-start.4
  9.6 15.2 %copy-start.45 = (f32[768]{0:T(1024)}, f32[768]{0:T(1024)S(1)}, u32[]{:S(2)}) copy-start(f32[768]{0:T(1024)S(1)} %fusion.70) | copy-start | bytes 9220
  10.3 14.5 %copy-start.42 = (f32[1536]{0:T(1024)}, f32[1536]{0:T(1024)S(1)}, u32[]{:S(2)}) copy-start(f32[1536]{0:T(1024)S(1)} %convert_element_type.141) | copy-start | bytes 18436
  24.9 4.3 copy-start.7
  24.9 4.3 copy-start.36
  30.3 14.3 %copy-start.40 = (bf16[768,384]{0,1:T(8,128)(2,1)}, bf16[768,384]{0,1:T(8,128)(2,1)S(1)}, u32[]{:S(2)}) copy-start(bf16[768,384]{0,1:T(8,128)(2,1)S(1)} %convolution_convert_fusion) | copy-start | bytes 1769476
  44.7 6.5 copy-start.38
  58.0 312.7 %all-reduce.5.cloned.1.call-start = ((), (), s32[]{:S(2)}) async-start(), calls=%async_computation.5 | async-start | bytes 9437184 | tf_op jit(solution)/shard_map/psum | solution.py:173
  269.1 342.9 %all-reduce.7.cloned.1.call-start = ((), (), s32[]{:S(2)}) async-start(), calls=%async_computation.11 | async-start | bytes 18874368 | tf_op jit(solution)/shard_map/psum | solution.py:152
  370.6 5.1 copy-start.10
  370.6 5.9 copy-start.29
  376.5 3.7 copy-start.34
  376.5 3.7 copy-start.35
  376.5 6.4 slice-start
  376.5 7.8 slice-start.1
  376.5 9.0 slice-start.2
  380.2 5.9 slice-start.3
  380.2 5.9 copy-start.41
  392.7 9.8 copy-start.12
  392.7 9.8 copy-start.14
  434.5 334.4 %reduce-scatter.15.cloned.1.call-start = ((), (), s32[]{:S(2)}) async-start(), calls=%async_computation.10 | async-start | bytes 12976128
  436.1 6.2 copy-start.54
  470.1 351.0 %reduce-scatter.13.cloned.1.call-start = ((), (), s32[]{:S(2)}) async-start(), calls=%async_computation.9 | async-start | bytes 10543104
  667.5 6.5 copy-start.30
  667.6 236.6 %reduce-scatter.9.cloned.1.call-start = ((), (), s32[]{:S(2)}) async-start(), calls=%async_computation.6 | async-start | bytes 2433024 | tf_op jit(solution)/shard_map/reduce_scatter | solution.py:242
  674.0 320.2 %reduce-scatter.11.cloned.1.call-start = ((), (), s32[]{:S(2)}) async-start(), calls=%async_computation.7 | async-start | bytes 6488064 | tf_op jit(solution)/shard_map/reduce_scatter | solution.py:244
  680.4 78.7 %copy-start.48 = (f32[768]{0:T(1024)S(1)}, f32[768]{0:T(1024)}, u32[]{:S(2)}) copy-start(f32[768]{0:T(1024)} %copy-done.47) | copy-start | bytes 9220
  755.2 12.3 %all-to-all-start = ((f32[32,1,22]{2,1,0:T(1,128)}), f32[32,1,22]{2,1,0:T(1,128)S(1)}, u32[]{:S(2)}, u32[]{:S(2)}) async-start(f32[32,1,22]{2,1,0:T(1,128)} %broadcast_in_dim.38), calls=%async_computation | async-start | bytes 32768 | tf_op jit(solution)/shard_map/all_to_all | solution.py:34
  759.1 235.1 %copy-start.1 = (bf16[1024,1536]{1,0:T(8,128)(2,1)S(1)}, bf16[1024,1536]{1,0:T(8,128)(2,1)}, u32[]{:S(2)}) copy-start(bf16[1024,1536]{1,0:T(8,128)(2,1)} %param.31) | copy-start | bytes 9437188
  (36 other events, 77.3 us)
Sparse Core Ops, SparseCore 0:
  58.1 174.8 all-gather.2
  269.2 101.3 all-reduce.4
  434.6 177.3 all-reduce.6
  615.7 104.4 reduce-scatter.14
  724.4 96.7 reduce-scatter.12
  825.5 78.5 reduce-scatter.8
  908.5 85.6 reduce-scatter.10
